TPU v7x, 32 devices: a whole 2x2x4 slice. The times are simulated.
32 devices in a mesh: rep: 4 (over z), shard: 8 (over y, x, core).
Axes of the slice: x: 2, y: 2, z: 4, core: 2. Of those that a mesh axis runs over, the one named last changes fastest.
Arguments:
- tokens: bfloat16 [4096, 2048], P(('rep', 'shard')), may hold values from -6 to 6
- attn_gain: float32 [2048], replicated, may hold values from 0.5 to 1.5
- query_weight: bfloat16 [2048, 2048], P('shard'), may hold values from -0.5 to 0.5
- key_weight: bfloat16 [2048, 512], P('shard'), may hold values from -0.5 to 0.5
- value_weight: bfloat16 [2048, 512], P('shard'), may hold values from -0.5 to 0.5
- output_weight: bfloat16 [2048, 2048], P('shard'), may hold values from -1 to 1
- ffn_gain: float32 [2048], replicated, may hold values from 0.5 to 1.5
- gate_weight: bfloat16 [2048, 8192], P('shard'), may hold values from -0.125 to 0.125
- up_weight: bfloat16 [2048, 8192], P('shard'), may hold values from -0.125 to 0.125
- down_weight: bfloat16 [8192, 2048], P('shard'), may hold values from -0.25 to 0.25
- dealing: int32 [4, 1024], P('rep'), may hold values from 0 to 1023, each once within a row
- lengths: int32 [4, 3], P('rep'), may hold values from 1 to 768, 1024 in all within a row
- cotangent: bfloat16 [4096, 2048], P(('rep', 'shard')), may hold values from -6 to 6
Outputs:
- layer_output: bfloat16 [4096, 2048], P(('rep', 'shard'))
- tokens_grad: float32 [4096, 2048], P(('rep', 'shard'))
- attn_gain_grad: float32 [2048], replicated
- query_weight_grad: float32 [2048, 2048], P('shard')
- key_weight_grad: float32 [2048, 512], P('shard')
- value_weight_grad: float32 [2048, 512], P('shard')
- output_weight_grad: float32 [2048, 2048], P('shard')
- ffn_gain_grad: float32 [2048], replicated
- gate_weight_grad: float32 [2048, 8192], P('shard')
- up_weight_grad: float32 [2048, 8192], P('shard')
- down_weight_grad: float32 [8192, 2048], P('shard')
Inputs may be any that keep to these rules, and one draw needn't show every extreme that they name: Each row of dealing is a permutation of 0 to 1023. Each row of lengths sums to 1024 and holds one length of exactly 768.
All inputs are finite; a program needn't handle non-finite values.
Results may differ from a plain program's by a relative error of at most 0.023.
Values may be sent and summed in bfloat16 or wider, within the bound.
A program may use at most 640 MiB of HBM per device.

v0:
```python
import jax
import jax.numpy as jnp
from jax import lax
from jax.sharding import PartitionSpec as P

HEADS = 32
KV_HEADS = 8
HEAD = 64
EPSILON = 1e-05
RESIDUAL_SCALE = 0.22
SCORE_SCALE = 0.015625
ROPE_BASE = 10000000.0
MASKED = -1e30


def rms_scale(hidden, gain_vector):
    return (
        hidden
        * lax.rsqrt(jnp.mean(hidden * hidden, axis=-1, keepdims=True) + EPSILON)
        * gain_vector
    )


def places(packed_index, seq_lengths):
    seq_ends = jnp.cumsum(seq_lengths)
    starts = seq_ends - seq_lengths
    segment = jnp.sum((packed_index[:, None] >= seq_ends[None, :]).astype(jnp.int32), axis=1)
    chosen = segment[:, None] == jnp.arange(seq_lengths.shape[0], dtype=jnp.int32)[None, :]
    position = packed_index - jnp.sum(jnp.where(chosen, starts[None, :], 0), axis=1)
    return (segment, position)


def angles(position, half_width):
    frequency = ROPE_BASE ** (
        -(jnp.arange(half_width, dtype=jnp.float32) * 2.0) / (2.0 * half_width)
    )
    turned = position.astype(jnp.float32)[:, None] * frequency[None, :]
    return (jnp.cos(turned)[:, None, :], jnp.sin(turned)[:, None, :])


def rotate(values, cosine, sine_table):
    half_width = values.shape[-1] // 2
    first_half = values[..., :half_width]
    second = values[..., half_width:]
    return jnp.concatenate(
        [first_half * cosine - second * sine_table, second * cosine + first_half * sine_table],
        axis=-1,
    )


def unrotate(values, cosine, sine_table):
    half_width = values.shape[-1] // 2
    first_half = values[..., :half_width]
    second = values[..., half_width:]
    return jnp.concatenate(
        [first_half * cosine + second * sine_table, second * cosine - first_half * sine_table],
        axis=-1,
    )


def picker(wanted, running, shard_piece):
    inside = (wanted >= 0) & (wanted < shard_piece.shape[0])
    picked = jnp.take(shard_piece, jnp.clip(wanted, 0, shard_piece.shape[0] - 1), axis=0)
    return running + jnp.where(inside[:, None], picked, jnp.zeros_like(picked))


def add_rows(inputs, shard_piece):
    return jnp.dot(inputs, shard_piece, preferred_element_type=jnp.float32)


def times_transposed(gradient, shard_piece):
    return lax.dot_general(
        gradient, shard_piece, (((1,), (1,)), ((), ())), preferred_element_type=jnp.float32
    )


def single_rows(inputs, weight):
    return add_rows(inputs, lax.all_gather(weight, "shard", axis=0, tiled=True))


def single_cols(gradient, weight):
    return times_transposed(gradient, lax.all_gather(weight, "shard", axis=0, tiled=True))


def spread(inputs, gradient):
    return lax.psum_scatter(
        lax.dot_general(
            inputs, gradient, (((0,), (0,)), ((), ())), preferred_element_type=jnp.float32
        ).astype(jnp.bfloat16),
        "shard",
        scatter_dimension=0,
        tiled=True,
    ).astype(jnp.float32)


def block_scores(queries, key_block, query_segment, query_position, key_segment, key_position):
    raw_scores = jnp.einsum(
        "rkgd,ckd->kgrc", queries, key_block, preferred_element_type=jnp.float32
    )
    allowed = (key_segment[None, :] == query_segment[:, None]) & (
        key_position[None, :] <= query_position[:, None]
    )
    return (SCORE_SCALE * raw_scores, allowed)


def per_device(
    tokens,
    attn_gain,
    query_weight,
    key_weight,
    value_weight,
    output_weight,
    ffn_gain,
    gate_weight,
    up_weight,
    down_weight,
    dealing,
    lengths,
    cotangent,
):
    local_rows = tokens.shape[0]
    model_width = tokens.shape[1]
    group_rows = local_rows * lax.axis_size("shard")
    kv_count = KV_HEADS
    head_width = HEAD
    per_group = HEADS // KV_HEADS
    here_index = lax.axis_index("shard")
    order_row = dealing[0]
    key_segment, key_position = places(order_row, lengths[0])
    query_segment = lax.dynamic_slice_in_dim(key_segment, here_index * local_rows, local_rows)
    query_position = lax.dynamic_slice_in_dim(key_position, here_index * local_rows, local_rows)
    my_tokens = lax.dynamic_slice_in_dim(order_row, here_index * local_rows, local_rows)
    cosine, sine_table = angles(query_position, head_width // 2)
    placed = picker(
        my_tokens,
        jnp.zeros((local_rows, model_width), jnp.bfloat16),
        lax.all_gather(tokens, "shard", axis=0, tiled=True),
    )
    hidden = placed.astype(jnp.float32)
    normed = rms_scale(hidden, attn_gain).astype(jnp.bfloat16)
    shard_pieces = (
        lax.all_gather(query_weight, "shard", axis=0, tiled=True),
        lax.all_gather(key_weight, "shard", axis=0, tiled=True),
        lax.all_gather(value_weight, "shard", axis=0, tiled=True),
    )
    query_pre = add_rows(normed, shard_pieces[0])
    key_pre = add_rows(normed, shard_pieces[1])
    value_pre = add_rows(normed, shard_pieces[2])
    queries = (
        rotate(query_pre.reshape(local_rows, HEADS, head_width), cosine, sine_table)
        .astype(jnp.bfloat16)
        .reshape(local_rows, kv_count, per_group, head_width)
    )
    key_local = (
        rotate(key_pre.reshape(local_rows, kv_count, head_width), cosine, sine_table)
        .astype(jnp.bfloat16)
        .reshape(local_rows, kv_count * head_width)
    )
    value_local = value_pre.astype(jnp.bfloat16)
    key_all, value_all = (
        lax.all_gather(key_local, "shard", axis=0, tiled=True),
        lax.all_gather(value_local, "shard", axis=0, tiled=True),
    )
    block_rows = 4 * local_rows
    block_count = group_rows // block_rows
    key_blocks = key_all.reshape(block_count, block_rows, kv_count, head_width)
    value_blocks = value_all.reshape(block_count, block_rows, kv_count, head_width)
    segment_blocks = key_segment.reshape(block_count, block_rows)
    position_blocks = key_position.reshape(block_count, block_rows)

    def gather_stats(running, block_item):
        running_top, running_sum = running
        key_block, segment_block, position_block = block_item
        scaled, allowed = block_scores(
            queries, key_block, query_segment, query_position, segment_block, position_block
        )
        masked_scores = jnp.where(allowed, scaled, MASKED)
        new_top = jnp.maximum(running_top, jnp.max(masked_scores, axis=-1))
        exponent = jnp.where(allowed, jnp.exp(masked_scores - new_top[..., None]), 0.0)
        running_sum = running_sum * jnp.exp(running_top - new_top) + jnp.sum(exponent, axis=-1)
        return ((new_top, running_sum), None)

    start_top = jnp.full((kv_count, per_group, local_rows), MASKED, jnp.float32)
    start_sum = jnp.zeros((kv_count, per_group, local_rows), jnp.float32)
    (score_top, score_sum), unused_stats = lax.scan(
        gather_stats, (start_top, start_sum), (key_blocks, segment_blocks, position_blocks)
    )
    log_total = score_top + jnp.log(score_sum)

    def weigh_values(running, block_item):
        upper_part, lower_part = running
        key_block, value_block, segment_block, position_block = block_item
        scaled, allowed = block_scores(
            queries, key_block, query_segment, query_position, segment_block, position_block
        )
        probabilities = jnp.where(allowed, jnp.exp(scaled - log_total[..., None]), 0.0)
        probs_high = probabilities.astype(jnp.bfloat16)
        probs_rest = (probabilities - probs_high.astype(jnp.float32)).astype(jnp.bfloat16)
        upper_part = upper_part + jnp.einsum(
            "kgrc,ckd->rkgd", probs_high, value_block, preferred_element_type=jnp.float32
        )
        lower_part = lower_part + jnp.einsum(
            "kgrc,ckd->rkgd", probs_rest, value_block, preferred_element_type=jnp.float32
        )
        return ((upper_part, lower_part), None)

    empty_heads = jnp.zeros((local_rows, kv_count, per_group, head_width), jnp.float32)
    (upper_part, lower_part), unused_weigh = lax.scan(
        weigh_values,
        (empty_heads, empty_heads),
        (key_blocks, value_blocks, segment_blocks, position_blocks),
    )
    attention = upper_part.astype(jnp.bfloat16).reshape(local_rows, model_width)
    attn_branch = single_rows(attention, output_weight)
    middle = hidden + RESIDUAL_SCALE * attn_branch
    normed_ffn = rms_scale(middle, ffn_gain).astype(jnp.bfloat16)
    shard_pieces = (
        lax.all_gather(gate_weight, "shard", axis=0, tiled=True),
        lax.all_gather(up_weight, "shard", axis=0, tiled=True),
    )
    gate_pre = add_rows(normed_ffn, shard_pieces[0])
    up_pre = add_rows(normed_ffn, shard_pieces[1])
    activated = (jax.nn.silu(gate_pre) * up_pre).astype(jnp.bfloat16)
    down_out = single_rows(activated, down_weight)
    layer_output = (middle + RESIDUAL_SCALE * down_out).astype(jnp.bfloat16)
    out_grad = cotangent.astype(jnp.float32)
    down_grad = (RESIDUAL_SCALE * out_grad).astype(jnp.bfloat16)
    down_weight_part = spread(activated, down_grad)
    act_grad = single_cols(down_grad, down_weight)
    unused_value, silu_pull = jax.vjp(
        lambda gate_in, up_in: jax.nn.silu(gate_in) * up_in, gate_pre, up_pre
    )
    gate_grad, up_grad = silu_pull(act_grad)
    gate_grad = gate_grad.astype(jnp.bfloat16)
    up_grad = up_grad.astype(jnp.bfloat16)
    gate_weight_part = spread(normed_ffn, gate_grad)
    up_weight_part = spread(normed_ffn, up_grad)
    shard_pieces = lax.all_gather((gate_weight, up_weight), "shard", axis=0, tiled=True)
    normed_ffn_grad = times_transposed(gate_grad, shard_pieces[0]) + times_transposed(
        up_grad, shard_pieces[1]
    )
    unused_norm, ffn_pull = jax.vjp(rms_scale, middle, ffn_gain)
    middle_part, ffn_gain_part = ffn_pull(normed_ffn_grad)
    middle_grad = out_grad + middle_part
    branch_grad = (RESIDUAL_SCALE * middle_grad).astype(jnp.bfloat16)
    output_weight_part = spread(attention, branch_grad)
    attention_grad = single_cols(branch_grad, output_weight)
    attention_grad = attention_grad.astype(jnp.bfloat16).reshape(
        local_rows, kv_count, per_group, head_width
    )
    row_delta = jnp.einsum(
        "rkgd,rkgd->kgr", attention_grad.astype(jnp.float32), upper_part + lower_part
    )

    def backward_block(query_grad, block_item):
        key_block, value_block, segment_block, position_block = block_item
        scaled, allowed = block_scores(
            queries, key_block, query_segment, query_position, segment_block, position_block
        )
        probabilities = jnp.where(allowed, jnp.exp(scaled - log_total[..., None]), 0.0)
        probs_grad = jnp.einsum(
            "rkgd,ckd->kgrc", attention_grad, value_block, preferred_element_type=jnp.float32
        )
        score_grad = (probabilities * (probs_grad - row_delta[..., None])).astype(jnp.bfloat16)
        query_grad = query_grad + SCORE_SCALE * jnp.einsum(
            "kgrc,ckd->rkgd", score_grad, key_block, preferred_element_type=jnp.float32
        )
        key_part = SCORE_SCALE * jnp.einsum(
            "kgrc,rkgd->ckd", score_grad, queries, preferred_element_type=jnp.float32
        )
        value_part = jnp.einsum(
            "kgrc,rkgd->ckd",
            probabilities.astype(jnp.bfloat16),
            attention_grad,
            preferred_element_type=jnp.float32,
        )
        return (query_grad, (key_part, value_part))

    query_grad, (key_parts, value_parts) = lax.scan(
        backward_block, empty_heads, (key_blocks, value_blocks, segment_blocks, position_blocks)
    )
    key_sum, value_sum = (
        lax.psum_scatter(
            key_parts.reshape(group_rows, kv_count * head_width).astype(jnp.bfloat16),
            "shard",
            scatter_dimension=0,
            tiled=True,
        ).astype(jnp.float32),
        lax.psum_scatter(
            value_parts.reshape(group_rows, kv_count * head_width).astype(jnp.bfloat16),
            "shard",
            scatter_dimension=0,
            tiled=True,
        ).astype(jnp.float32),
    )
    query_pre_grad = (
        unrotate(query_grad.reshape(local_rows, HEADS, head_width), cosine, sine_table)
        .reshape(local_rows, model_width)
        .astype(jnp.bfloat16)
    )
    key_pre_grad = (
        unrotate(key_sum.reshape(local_rows, kv_count, head_width), cosine, sine_table)
        .reshape(local_rows, kv_count * head_width)
        .astype(jnp.bfloat16)
    )
    value_pre_grad = value_sum.astype(jnp.bfloat16)
    query_weight_part = spread(normed, query_pre_grad)
    key_weight_part = spread(normed, key_pre_grad)
    value_weight_part = spread(normed, value_pre_grad)
    shard_pieces = lax.all_gather(
        (query_weight, key_weight, value_weight), "shard", axis=0, tiled=True
    )
    normed_grad = (
        times_transposed(query_pre_grad, shard_pieces[0])
        + times_transposed(key_pre_grad, shard_pieces[1])
        + times_transposed(value_pre_grad, shard_pieces[2])
    )
    unused_first, attn_pull = jax.vjp(rms_scale, hidden, attn_gain)
    hidden_part, attn_gain_part = attn_pull(normed_grad)
    dealt_grad = middle_grad + hidden_part
    inverse = (
        jnp.zeros((group_rows,), jnp.int32)
        .at[order_row]
        .set(jnp.arange(group_rows, dtype=jnp.int32))
    )
    wanted_slots = lax.dynamic_slice_in_dim(inverse, here_index * local_rows, local_rows)
    tokens_grad = picker(
        wanted_slots,
        jnp.zeros((local_rows, model_width), jnp.float32),
        lax.all_gather(dealt_grad.astype(jnp.bfloat16), "shard", axis=0, tiled=True).astype(
            jnp.float32
        ),
    )
    summed = (
        lax.psum(query_weight_part.astype(jnp.bfloat16), "rep").astype(jnp.float32),
        lax.psum(key_weight_part.astype(jnp.bfloat16), "rep").astype(jnp.float32),
        lax.psum(value_weight_part.astype(jnp.bfloat16), "rep").astype(jnp.float32),
        lax.psum(output_weight_part.astype(jnp.bfloat16), "rep").astype(jnp.float32),
        lax.psum(gate_weight_part.astype(jnp.bfloat16), "rep").astype(jnp.float32),
        lax.psum(up_weight_part.astype(jnp.bfloat16), "rep").astype(jnp.float32),
        lax.psum(down_weight_part.astype(jnp.bfloat16), "rep").astype(jnp.float32),
    )
    attn_gain_grad, ffn_gain_grad = lax.psum((attn_gain_part, ffn_gain_part), ("rep", "shard"))
    return (
        layer_output,
        tokens_grad,
        attn_gain_grad,
        summed[0],
        summed[1],
        summed[2],
        summed[3],
        ffn_gain_grad,
        summed[4],
        summed[5],
        summed[6],
    )


def solution(mesh):
    return jax.shard_map(
        per_device,
        mesh=mesh,
        in_specs=(
            P(("rep", "shard"), None),
            P(),
            P("shard", None),
            P("shard", None),
            P("shard", None),
            P("shard", None),
            P(),
            P("shard", None),
            P("shard", None),
            P("shard", None),
            P("rep", None),
            P("rep", None),
            P(("rep", "shard"), None),
        ),
        out_specs=(
            P(("rep", "shard"), None),
            P(("rep", "shard"), None),
            P(),
            P("shard", None),
            P("shard", None),
            P("shard", None),
            P("shard", None),
            P(),
            P("shard", None),
            P("shard", None),
            P("shard", None),
        ),
        check_vma=False,
    )
```

profile of v0, /device:TPU:0, one launch (start us, length us, event | category | flops | bytes accessed | tf_op | source)
XLA Modules:
  0.0 2409.0 jit_solution(6717161342337709093)
XLA Ops:
  11.5 37.9 %all-gather.12.cloned.1.call-done = bf16[1024,2048]{1,0:T(8,128)(2,1)} async-done(((bf16[128,2048]{1,0:T(8,128)(2,1)}), bf16[1024,2048]{1,0:T(8,128)(2,1)}) %all-gather.12.cloned.1.call-update) | async-done | bytes 4194320 | tf_op jit(solution)/shard_map/all_gather | solution.py:137
  53.9 25.3 %all-gather.14.cloned.1.call-done = bf16[2048,512]{1,0:T(8,128)(2,1)} async-done(((bf16[256,512]{1,0:T(8,128)(2,1)}), bf16[2048,512]{1,0:T(8,128)(2,1)}) %all-gather.14.cloned.1.call-update) | async-done | bytes 2097168 | tf_op jit(solution)/shard_map/all_gather | solution.py:144
  82.7 26.3 %all-gather.18.cloned.1.call-done = bf16[2048,512]{1,0:T(8,128)(2,1)} async-done(((bf16[256,512]{1,0:T(8,128)(2,1)}), bf16[2048,512]{1,0:T(8,128)(2,1)}) %all-gather.18.cloned.1.call-update) | async-done | bytes 2097168 | tf_op jit(solution)/shard_map/all_gather | solution.py:143
  117.7 17.2 all-gather.16.cloned.1.call-done
  142.1 18.7 all-gather.20.cloned.1.call-done
  164.8 52.1 %all-gather.22.cloned.1.call-done = bf16[2048,2048]{1,0:T(8,128)(2,1)} async-done(((bf16[256,2048]{1,0:T(8,128)(2,1)}), bf16[2048,2048]{1,0:T(8,128)(2,1)}) %all-gather.22.cloned.1.call-update) | async-done | bytes 8388624 | tf_op jit(solution)/shard_map/all_gather | solution.py:142
  217.0 6.9 fusion.103
  224.1 19.2 while.41
  224.3 4.8 fusion.180
  229.1 4.6 select_reduce_fusion.3
  234.0 4.7 fusion.180
  243.3 30.6 %while.42 = (s32[]{:T(128)}, f32[128,8,4,64]{0,3,2,1:T(8,128)S(1)}, f32[128,8,4,64]{0,3,2,1:T(8,128)}, bf16[2,512,8,64]{1,3,2,0:T(8,128)(2,1)}, s32[2,512]{1,0:T...) while((s32[]{:T(128)}, f32[128,8,4,64]{0,3,2,1:T(8,128)S(1)}, ...), condition=%wide.region_9.10_spmd.clone, body=%wide.region_8.9_spmd.clone.sunk | while | flops 829620224 | bytes 77837592 | solution.py:208
  243.5 5.5 fusion.187
  249.2 5.6 fusion.188
  259.1 4.7 fusion.187
  264.0 5.7 fusion.188
  275.1 5.1 multiply_reduce_fusion.2
  281.3 154.7 %all-gather.26.cloned.1.call-done = bf16[2048,8192]{1,0:T(8,128)(2,1)} async-done(((bf16[256,8192]{1,0:T(8,128)(2,1)}), bf16[2048,8192]{1,0:T(8,128)(2,1)}) %all-gather.26.cloned.1.call-update) | async-done | bytes 33554448 | tf_op jit(solution)/shard_map/all_gather | solution.py:218
  436.0 19.2 fusion.109
  455.2 143.5 %all-gather.28.cloned.1.call-done = bf16[2048,8192]{1,0:T(8,128)(2,1)} async-done(((bf16[256,8192]{1,0:T(8,128)(2,1)}), bf16[2048,8192]{1,0:T(8,128)(2,1)}) %all-gather.28.cloned.1.call-update) | async-done | bytes 33554448 | tf_op jit(solution)/shard_map/all_gather | solution.py:219
  598.7 19.3 fusion.110
  618.0 143.3 %all-gather.30.cloned.1.call-done = bf16[8192,2048]{1,0:T(8,128)(2,1)} async-done(((bf16[1024,2048]{1,0:T(8,128)(2,1)}), bf16[8192,2048]{1,0:T(8,128)(2,1)}) %all-gather.30.cloned.1.call-update) | async-done | bytes 33554448 | tf_op jit(solution)/shard_map/all_gather | solution.py:78
  761.3 21.2 multiply_convert_fusion
  782.4 16.3 fusion.111
  798.7 18.2 multiply_reduce_fusion
  819.9 7.1 convolution_convert_fusion.7
  831.0 40.0 %while.43 = (s32[]{:T(128)}, f32[128,8,4,64]{0,3,2,1:T(8,128)S(1)}, bf16[2,512,8,64]{1,3,2,0:T(8,128)(2,1)}, bf16[2,512,8,64]{1,3,2,0:T(8,128)(2,1)}, bf16[2,512...) while((s32[]{:T(128)}, f32[128,8,4,64]{0,3,2,1:T(8,128)S(1)}, ...), condition=%wide.region_14.15_spmd.clone, body=%wide.region_13.14_spmd.clone.sunk | while | flops 1364393984 | bytes 129758592 | solution.py:279
  843.5 5.2 fusion.203
  863.3 5.2 fusion.203
  886.2 28.5 %reduce-scatter.28.cloned.1.call-done = bf16[128,512]{1,0:T(8,128)(2,1)} async-done(((bf16[1024,512]{1,0:T(8,128)(2,1)}), bf16[128,512]{1,0:T(8,128)(2,1)}) %reduce-scatter.28.cloned.1.call-update) | async-done | bytes 131088
  918.2 36.2 %reduce-scatter.30.cloned.1.call-done = bf16[128,512]{1,0:T(8,128)(2,1)} async-done(((bf16[1024,512]{1,0:T(8,128)(2,1)}), bf16[128,512]{1,0:T(8,128)(2,1)}) %reduce-scatter.30.cloned.1.call-update) | async-done | bytes 131088
  958.1 5.9 convolution_convert_fusion.4
  964.1 5.7 convolution_convert_fusion.3
  969.9 15.6 convolution_convert_fusion.1
  985.6 15.8 convolution_convert_fusion
  1002.4 15.7 convolution_convert_fusion.2
  1018.5 6.4 fusion.112
  1028.2 15.5 reduce-scatter.18.cloned.1.call-done
  1043.7 75.2 %reduce-scatter.14.cloned.1.call-done = bf16[256,2048]{1,0:T(8,128)(2,1)} async-done(((bf16[2048,2048]{1,0:T(8,128)(2,1)}), bf16[256,2048]{1,0:T(8,128)(2,1)}) %reduce-scatter.14.cloned.1.call-update) | async-done | bytes 1048592 | tf_op jit(solution)/shard_map/reduce_scatter | solution.py:86
  1118.9 75.6 %reduce-scatter.20.cloned.1.call-done = bf16[256,2048]{1,0:T(8,128)(2,1)} async-done(((bf16[2048,2048]{1,0:T(8,128)(2,1)}), bf16[256,2048]{1,0:T(8,128)(2,1)}) %reduce-scatter.20.cloned.1.call-update) | async-done | bytes 1048592 | tf_op jit(solution)/shard_map/reduce_scatter | solution.py:86
  1194.5 208.7 %reduce-scatter.22.cloned.1.call-done = bf16[256,8192]{1,0:T(8,128)(2,1)} async-done(((bf16[2048,8192]{1,0:T(8,128)(2,1)}), bf16[256,8192]{1,0:T(8,128)(2,1)}) %reduce-scatter.22.cloned.1.call-update) | async-done | bytes 4194320 | tf_op jit(solution)/shard_map/reduce_scatter | solution.py:86
  1403.2 209.1 %reduce-scatter.24.cloned.1.call-done = bf16[256,8192]{1,0:T(8,128)(2,1)} async-done(((bf16[2048,8192]{1,0:T(8,128)(2,1)}), bf16[256,8192]{1,0:T(8,128)(2,1)}) %reduce-scatter.24.cloned.1.call-update) | async-done | bytes 4194320 | tf_op jit(solution)/shard_map/reduce_scatter | solution.py:86
  1612.3 208.8 %reduce-scatter.26.cloned.1.call-done = bf16[1024,2048]{1,0:T(8,128)(2,1)} async-done(((bf16[8192,2048]{1,0:T(8,128)(2,1)}), bf16[1024,2048]{1,0:T(8,128)(2,1)}) %reduce-scatter.26.cloned.1.call-update) | async-done | bytes 4194320 | tf_op jit(solution)/shard_map/reduce_scatter | solution.py:86
  1825.7 14.4 fusion.76
  1840.0 39.9 %all-reduce = (f32[2048]{0:T(1024)}, f32[2048]{0:T(1024)}) all-reduce(f32[2048]{0:T(1024)S(1)} %get-tuple-element.438, f32[2048]{0:T(1024)S(1)} %copy-done.37), channel_id=1, replica_groups=mesh['rep'=4,'shard'=8] {'rep','shard'}, use_global_device_ids=true, to_apply=%region_19.20 | all-reduce | flops 4096 | bytes 32768 | tf_op jit(solution)/shard_map/psum | solution.py:343
  1879.9 6.7 convert_element_type.176
  1886.6 4.8 gather_fusion.1
  1892.6 486.6 %all-reduce.4.cloned.1.call-done = (bf16[256,2048]{1,0:T(8,128)(2,1)}, bf16[256,512]{1,0:T(8,128)(2,1)}, bf16[256,512]{1,0:T(8,128)(2,1)}, bf16[256,2048]{1,0:T(...) async-done(((bf16[256,2048]{1,0:T(8,128)(2,1)}, bf16[256,512]{1,0:T(8,128)(2,1)}, bf16[256,512]{1,0:T(8,128)(2,1)}, ...) | async-done | bytes 15204368 | tf_op jit(solution)/shard_map/psum | solution.py:335
  (258 shorter events, 139.5 us)
Async XLA Ops:
  7.2 75.1 %copy-start.35 = (s32[1,1024]{1,0:T(1,128)S(1)}, s32[1,1024]{1,0:T(1,128)}, u32[]{:S(2)}) copy-start(s32[1,1024]{1,0:T(1,128)} %param.29) | copy-start | bytes 12292
  7.2 101.9 %copy-start.28 = (f32[2048]{0:T(1024)S(1)}, f32[2048]{0:T(1024)}, u32[]{:S(2)}) copy-start(f32[2048]{0:T(1024)} %param.20) | copy-start | bytes 24580
  7.2 74.9 %copy-start.42 = (s32[1,3]{1,0:T(1,128)S(1)}, s32[1,3]{1,0:T(1,128)}, u32[]{:S(2)}) copy-start(s32[1,3]{1,0:T(1,128)} %param.30) | copy-start | bytes 40
  7.2 42.2 %all-gather.12.cloned.1.call-start = ((), (), s32[]{:S(2)}) async-start(), calls=%async_computation.9 | async-start | bytes 4718592 | tf_op jit(solution)/shard_map/all_gather | solution.py:137
  7.9 71.3 %all-gather.14.cloned.1.call-start = ((), (), s32[]{:S(2)}) async-start(), calls=%async_computation.10 | async-start | bytes 2359296 | tf_op jit(solution)/shard_map/all_gather | solution.py:144
  8.7 100.4 %all-gather.18.cloned.1.call-start = ((), (), s32[]{:S(2)}) async-start(), calls=%async_computation.12 | async-start | bytes 2359296 | tf_op jit(solution)/shard_map/all_gather | solution.py:143
  9.4 125.5 %all-gather.16.cloned.1.call-start = ((), (), s32[]{:S(2)}) async-start(), calls=%async_computation.11 | async-start | bytes 1179648 | tf_op jit(solution)/shard_map/all_gather | solution.py:162
  53.9 28.6 %copy-start.40 = (f32[128]{0:T(128)}, f32[128]{0:T(128)S(1)}, u32[]{:S(2)}) copy-start(f32[128]{0:T(128)S(1)} %fusion.84) | copy-start | bytes 1540
  53.9 163.1 %copy-start.38 = (f32[128]{0:T(128)}, f32[128]{0:T(128)S(1)}, u32[]{:S(2)}) copy-start(f32[128]{0:T(128)S(1)} %fusion.94) | copy-start | bytes 1540
  82.0 78.8 %all-gather.20.cloned.1.call-start = ((), (), s32[]{:S(2)}) async-start(), calls=%async_computation.13 | async-start | bytes 1179648 | tf_op jit(solution)/shard_map/all_gather | solution.py:161
  82.7 141.2 %copy-start.30 = (f32[128,32]{0,1:T(8,128)}, f32[128,32]{0,1:T(8,128)S(1)}, u32[]{:S(2)}) copy-start(f32[128,32]{0,1:T(8,128)S(1)} %get-tuple-element.541) | copy-start | bytes 49156
  82.7 141.2 %copy-start.32 = (f32[128,32]{0,1:T(8,128)}, f32[128,32]{0,1:T(8,128)S(1)}, u32[]{:S(2)}) copy-start(f32[128,32]{0,1:T(8,128)S(1)} %get-tuple-element.542) | copy-start | bytes 49156
  112.4 104.6 %all-gather.22.cloned.1.call-start = ((), (), s32[]{:S(2)}) async-start(), calls=%async_computation.14 | async-start | bytes 9437184 | tf_op jit(solution)/shard_map/all_gather | solution.py:142
  113.0 162.0 %all-gather.24.cloned.1.call-start = ((), (), s32[]{:S(2)}) async-start(), calls=%async_computation.15 | async-start | bytes 9437184 | tf_op jit(solution)/shard_map/all_gather | solution.py:78
  113.7 322.2 %all-gather.26.cloned.1.call-start = ((), (), s32[]{:S(2)}) async-start(), calls=%async_computation.16 | async-start | bytes 37748736 | tf_op jit(solution)/shard_map/all_gather | solution.py:218
  114.5 484.2 %all-gather.28.cloned.1.call-start = ((), (), s32[]{:S(2)}) async-start(), calls=%async_computation.17 | async-start | bytes 37748736 | tf_op jit(solution)/shard_map/all_gather | solution.py:219
  115.2 646.0 %all-gather.30.cloned.1.call-start = ((), (), s32[]{:S(2)}) async-start(), calls=%async_computation.18 | async-start | bytes 37748736 | tf_op jit(solution)/shard_map/all_gather | solution.py:78
  115.8 799.0 %reduce-scatter.28.cloned.1.call-start = ((), (), s32[]{:S(2)}) async-start(), calls=%async_computation.27 | async-start | bytes 1179648
  280.2 518.5 %copy-start.4 = (f32[128,2048]{1,0:T(8,128)}, f32[128,2048]{1,0:T(8,128)S(1)}, u32[]{:S(2)}) copy-start(f32[128,2048]{1,0:T(8,128)S(1)} %get-tuple-element.544) | copy-start | bytes 3145732
  798.7 18.3 copy-start.19
  817.0 14.0 copy-start.3
  840.3 8.4 copy-start.1
  840.3 8.4 copy-start.16
  840.3 8.4 copy-start.23
  860.0 8.4 copy-start.1
  860.0 8.4 copy-start.16
  860.0 8.4 copy-start.23
  871.0 44.8 %copy-start.31 = (f32[128,32]{0,1:T(8,128)S(1)}, f32[128,32]{0,1:T(8,128)}, u32[]{:S(2)}) copy-start(f32[128,32]{0,1:T(8,128)} %copy-done.30) | copy-start | bytes 49156
  871.0 44.8 %copy-start.33 = (f32[128,32]{0,1:T(8,128)S(1)}, f32[128,32]{0,1:T(8,128)}, u32[]{:S(2)}) copy-start(f32[128,32]{0,1:T(8,128)} %copy-done.32) | copy-start | bytes 49156
  871.0 44.9 %copy-start.29 = (f32[2048]{0:T(1024)S(1)}, f32[2048]{0:T(1024)}, u32[]{:S(2)}) copy-start(f32[2048]{0:T(1024)} %param.20) | copy-start | bytes 24580
  871.0 44.9 %copy-start.39 = (f32[128]{0:T(128)S(1)}, f32[128]{0:T(128)}, u32[]{:S(2)}) copy-start(f32[128]{0:T(128)} %copy-done.38) | copy-start | bytes 1540
  878.6 75.8 %reduce-scatter.30.cloned.1.call-start = ((), (), s32[]{:S(2)}) async-start(), calls=%async_computation.28 | async-start | bytes 1179648
  886.2 142.0 %reduce-scatter.16.cloned.1.call-start = ((), (), s32[]{:S(2)}) async-start(), calls=%async_computation.21 | async-start | bytes 2359296 | tf_op jit(solution)/shard_map/reduce_scatter | solution.py:86
  918.1 125.5 %reduce-scatter.18.cloned.1.call-start = ((), (), s32[]{:S(2)}) async-start(), calls=%async_computation.22 | async-start | bytes 2359296 | tf_op jit(solution)/shard_map/reduce_scatter | solution.py:86
  957.6 161.2 %reduce-scatter.14.cloned.1.call-start = ((), (), s32[]{:S(2)}) async-start(), calls=%async_computation.20 | async-start | bytes 9437184 | tf_op jit(solution)/shard_map/reduce_scatter | solution.py:86
  964.0 230.5 %reduce-scatter.20.cloned.1.call-start = ((), (), s32[]{:S(2)}) async-start(), calls=%async_computation.23 | async-start | bytes 9437184 | tf_op jit(solution)/shard_map/reduce_scatter | solution.py:86
  969.8 433.3 %reduce-scatter.22.cloned.1.call-start = ((), (), s32[]{:S(2)}) async-start(), calls=%async_computation.24 | async-start | bytes 37748736 | tf_op jit(solution)/shard_map/reduce_scatter | solution.py:86
  985.6 626.7 %reduce-scatter.24.cloned.1.call-start = ((), (), s32[]{:S(2)}) async-start(), calls=%async_computation.25 | async-start | bytes 37748736 | tf_op jit(solution)/shard_map/reduce_scatter | solution.py:86
  1001.4 819.7 %reduce-scatter.26.cloned.1.call-start = ((), (), s32[]{:S(2)}) async-start(), calls=%async_computation.26 | async-start | bytes 37748736 | tf_op jit(solution)/shard_map/reduce_scatter | solution.py:86
  1018.2 8.6 copy-start.41
  1018.2 861.7 %all-gather.32.cloned.1.call-start = ((), (), s32[]{:S(2)}) async-start(), calls=%async_computation.19 | async-start | bytes 4718592 | tf_op jit(solution)/shard_map/all_gather | solution.py:330
  1028.1 793.1 %copy-start.36 = (s32[1,1024]{1,0:T(1,128)S(1)}, s32[1,1024]{1,0:T(1,128)}, u32[]{:S(2)}) copy-start(s32[1,1024]{1,0:T(1,128)} %param.29) | copy-start | bytes 12292
  1028.1 797.5 %copy-start.5 = (f32[128,2048]{1,0:T(8,128)S(1)}, f32[128,2048]{1,0:T(8,128)}, u32[]{:S(2)}) copy-start(f32[128,2048]{1,0:T(8,128)} %copy-done.4) | copy-start | bytes 3145732
  1028.1 797.5 %copy-start.9 = (bf16[128,8192]{1,0:T(8,128)(2,1)S(1)}, bf16[128,8192]{1,0:T(8,128)(2,1)}, u32[]{:S(2)}) copy-start(bf16[128,8192]{1,0:T(8,128)(2,1)} %get-tuple-element.531) | copy-start | bytes 6291460
  1028.1 1351.1 %all-reduce.4.cloned.1.call-start = ((), (), s32[]{:S(2)}) async-start(), calls=%async_computation.29 | async-start | bytes 30408704 | tf_op jit(solution)/shard_map/psum | solution.py:335
  1825.7 14.4 copy-start.37
  2379.2 9.5 copy-start.13
  2384.0 9.1 copy-start.12
  (27 other events, 119.1 us)
Sparse Core Ops, SparseCore 0:
  9.9 39.4 all-gather.11
  51.3 27.8 all-gather.13
  81.1 27.9 all-gather.17
  111.4 23.4 all-gather.15
  137.2 23.5 all-gather.19
  162.5 54.3 all-gather.21
  218.8 54.4 all-gather.23
  275.2 160.7 all-gather.25
  437.9 160.7 all-gather.27
  600.4 160.7 all-gather.29
  878.7 36.0 reduce-scatter.27
  918.4 35.9 reduce-scatter.29
  957.7 41.1 reduce-scatter.15
  1002.4 41.2 reduce-scatter.17
  1047.5 71.2 reduce-scatter.13
  1123.1 71.2 reduce-scatter.19
  1197.9 205.2 reduce-scatter.21
  1407.0 205.2 reduce-scatter.23
  1615.9 205.2 reduce-scatter.25
  1823.6 37.2 all-gather.31
  1864.7 514.4 all-reduce.3
where the time goes:
time: 2410 us
  waiting for transfers between devices  1970 us (82%)
  matrix products  272 us (11%)
  local copies, waits for them, and re-layouts  57.5 us (2%)
  other arithmetic  53.1 us (2%)
  blocking collectives  39.9 us (2%)
    reduce_scatter x7, waiting for transfers between devices, spread(): lax.psum_scatter(lax.dot_general(inputs, gradient, (((0,), (0,)), ((), ()...  793 us
    psum x1, waiting for transfers between devices, per_device(): lax.psum(query_weight_part.astype(jnp.bfloat16), 'rep').astype(jnp.float32)  487 us
    all_gather x1, waiting for transfers between devices, per_device(): lax.all_gather(gate_weight, 'shard', axis=0, tiled=True)  155 us
    all_gather x1, waiting for transfers between devices, per_device(): lax.all_gather(up_weight, 'shard', axis=0, tiled=True)  144 us
    all_gather x2, waiting for transfers between devices, single_rows(): return add_rows(inputs, lax.all_gather(weight, 'shard', axis=0, tiled=True))  143 us
    dot_general x7, matrix products, times_transposed(): lax.dot_general(gradient, shard_piece, (((1,), (1,)), ((), ())), preferre...  71.1 us
    unnamed x23, waiting for transfers between devices  70.2 us
    dot_general x7, matrix products, add_rows(): return jnp.dot(inputs, shard_piece, preferred_element_type=jnp.float32)  70.2 us
  transfers between devices with their start and end apart: 21, of which 18 were waited for; matrix products, arithmetic and copies ran while one was open for 10% of the time, Pallas kernels for 0%

commit v1 on v0

--- a/solution.py
+++ b/solution.py
@@ -332,7 +332,9 @@
         ),
     )
     summed = (
-        lax.psum(query_weight_part.astype(jnp.bfloat16), "rep").astype(jnp.float32),
+        jnp.sum(lax.all_gather(query_weight_part.astype(jnp.bfloat16), "rep"), axis=0).astype(
+            jnp.float32
+        ),
         lax.psum(key_weight_part.astype(jnp.bfloat16), "rep").astype(jnp.float32),
         lax.psum(value_weight_part.astype(jnp.bfloat16), "rep").astype(jnp.float32),
         lax.psum(output_weight_part.astype(jnp.bfloat16), "rep").astype(jnp.float32),

time: 2410 us -> 2460 us (1.021)
  waiting for transfers between devices: 1970 us -> 2010 us
    all_gather x0 -> x1, waiting for transfers between devices: none -> 50.5 us  [per_device(): lax.all_gather(query_weight_part.astype(jnp.bfloat16), 'rep')]
    unnamed x23 -> x24, waiting for transfers between devices: 70.2 us -> 63.8 us
  transfers between devices with their start and end apart: 21 -> 22, of which waited for: 18 -> 20; matrix products, arithmetic and copies ran while one was open for 10% -> 10% of each run, Pallas kernels for 0% -> 0%
where the time goes in v1:
time: 2460 us; the launch traced here: 2450 us
  waiting for transfers between devices  2010 us (82%)
  matrix products  274 us (11%)
  local copies, waits for them, and re-layouts  57.6 us (2%)
  other arithmetic  57 us (2%)
  blocking collectives  39.9 us (2%)
    reduce_scatter x7, waiting for transfers between devices, spread(): lax.psum_scatter(lax.dot_general(inputs, gradient, (((0,), (0,)), ((), ()...  797 us
    psum x1, waiting for transfers between devices, per_device(): lax.psum(key_weight_part.astype(jnp.bfloat16), 'rep').astype(jnp.float32)  478 us
    all_gather x1, waiting for transfers between devices, per_device(): lax.all_gather(gate_weight, 'shard', axis=0, tiled=True)  155 us
    all_gather x1, waiting for transfers between devices, per_device(): lax.all_gather(up_weight, 'shard', axis=0, tiled=True)  144 us
    all_gather x2, waiting for transfers between devices, single_rows(): return add_rows(inputs, lax.all_gather(weight, 'shard', axis=0, tiled=True))  143 us
    dot_general x7, matrix products, times_transposed(): lax.dot_general(gradient, shard_piece, (((1,), (1,)), ((), ())), preferre...  72 us
    dot_general x7, matrix products, add_rows(): return jnp.dot(inputs, shard_piece, preferred_element_type=jnp.float32)  70.2 us
    dot_general x7, matrix products, spread(): lax.dot_general(inputs, gradient, (((0,), (0,)), ((), ())), preferred_ele...  66 us
  transfers between devices with their start and end apart: 22, of which 20 were waited for; matrix products, arithmetic and copies ran while one was open for 10% of the time, Pallas kernels for 0%

profile of v1, /device:TPU:0, one launch (start us, length us, event | category | flops | bytes accessed | tf_op | source)
XLA Modules:
  0.0 2454.8 jit_solution(6213050016543146827)
XLA Ops:
  11.5 37.9 %all-gather.14.cloned.1.call-done = bf16[1024,2048]{1,0:T(8,128)(2,1)} async-done(((bf16[128,2048]{1,0:T(8,128)(2,1)}), bf16[1024,2048]{1,0:T(8,128)(2,1)}) %all-gather.14.cloned.1.call-update) | async-done | bytes 4194320 | tf_op jit(solution)/shard_map/all_gather | solution.py:137
  53.9 25.3 %all-gather.16.cloned.1.call-done = bf16[2048,512]{1,0:T(8,128)(2,1)} async-done(((bf16[256,512]{1,0:T(8,128)(2,1)}), bf16[2048,512]{1,0:T(8,128)(2,1)}) %all-gather.16.cloned.1.call-update) | async-done | bytes 2097168 | tf_op jit(solution)/shard_map/all_gather | solution.py:144
  82.7 26.3 %all-gather.20.cloned.1.call-done = bf16[2048,512]{1,0:T(8,128)(2,1)} async-done(((bf16[256,512]{1,0:T(8,128)(2,1)}), bf16[2048,512]{1,0:T(8,128)(2,1)}) %all-gather.20.cloned.1.call-update) | async-done | bytes 2097168 | tf_op jit(solution)/shard_map/all_gather | solution.py:143
  117.7 17.2 all-gather.18.cloned.1.call-done
  142.1 18.7 all-gather.22.cloned.1.call-done
  164.8 52.1 %all-gather.24.cloned.1.call-done = bf16[2048,2048]{1,0:T(8,128)(2,1)} async-done(((bf16[256,2048]{1,0:T(8,128)(2,1)}), bf16[2048,2048]{1,0:T(8,128)(2,1)}) %all-gather.24.cloned.1.call-update) | async-done | bytes 8388624 | tf_op jit(solution)/shard_map/all_gather | solution.py:142
  217.0 6.9 fusion.103
  224.1 19.2 while.41
  224.3 4.8 fusion.180
  243.3 30.6 %while.42 = (s32[]{:T(128)}, f32[128,8,4,64]{0,3,2,1:T(8,128)S(1)}, f32[128,8,4,64]{0,3,2,1:T(8,128)}, bf16[2,512,8,64]{1,3,2,0:T(8,128)(2,1)}, s32[2,512]{1,0:T...) while((s32[]{:T(128)}, f32[128,8,4,64]{0,3,2,1:T(8,128)S(1)}, ...), condition=%wide.region_9.10_spmd.clone, body=%wide.region_8.9_spmd.clone.sunk | while | flops 829620224 | bytes 77837592 | solution.py:208
  243.5 5.5 fusion.187
  249.3 5.6 fusion.188
  264.0 5.7 fusion.188
  275.1 5.1 multiply_reduce_fusion.2
  281.3 154.6 %all-gather.28.cloned.1.call-done = bf16[2048,8192]{1,0:T(8,128)(2,1)} async-done(((bf16[256,8192]{1,0:T(8,128)(2,1)}), bf16[2048,8192]{1,0:T(8,128)(2,1)}) %all-gather.28.cloned.1.call-update) | async-done | bytes 33554448 | tf_op jit(solution)/shard_map/all_gather | solution.py:218
  436.0 19.2 fusion.109
  455.2 143.5 %all-gather.30.cloned.1.call-done = bf16[2048,8192]{1,0:T(8,128)(2,1)} async-done(((bf16[256,8192]{1,0:T(8,128)(2,1)}), bf16[2048,8192]{1,0:T(8,128)(2,1)}) %all-gather.30.cloned.1.call-update) | async-done | bytes 33554448 | tf_op jit(solution)/shard_map/all_gather | solution.py:219
  598.7 19.3 fusion.110
  618.0 143.3 %all-gather.32.cloned.1.call-done = bf16[8192,2048]{1,0:T(8,128)(2,1)} async-done(((bf16[1024,2048]{1,0:T(8,128)(2,1)}), bf16[8192,2048]{1,0:T(8,128)(2,1)}) %all-gather.32.cloned.1.call-update) | async-done | bytes 33554448 | tf_op jit(solution)/shard_map/all_gather | solution.py:78
  761.3 21.4 multiply_convert_fusion
  782.7 16.3 fusion.111
  799.0 18.2 multiply_reduce_fusion
  820.2 7.1 convolution_convert_fusion.7
  831.3 39.7 %while.43 = (s32[]{:T(128)}, f32[128,8,4,64]{0,3,2,1:T(8,128)S(1)}, bf16[2,512,8,64]{1,3,2,0:T(8,128)(2,1)}, bf16[2,512,8,64]{1,3,2,0:T(8,128)(2,1)}, bf16[2,512...) while((s32[]{:T(128)}, f32[128,8,4,64]{0,3,2,1:T(8,128)S(1)}, ...), condition=%wide.region_14.15_spmd.clone, body=%wide.region_13.14_spmd.clone.sunk | while | flops 1364393984 | bytes 129758592 | solution.py:279
  843.5 5.2 fusion.203
  863.3 5.2 fusion.203
  886.5 5.9 convolution_convert_fusion.4
  892.7 22.1 reduce-scatter.28.cloned.1.call-done
  918.2 36.3 %reduce-scatter.30.cloned.1.call-done = bf16[128,512]{1,0:T(8,128)(2,1)} async-done(((bf16[1024,512]{1,0:T(8,128)(2,1)}), bf16[128,512]{1,0:T(8,128)(2,1)}) %reduce-scatter.30.cloned.1.call-update) | async-done | bytes 131088
  957.7 5.7 convolution_convert_fusion.3
  963.5 17.5 convolution_convert_fusion.1
  981.1 15.8 convolution_convert_fusion
  997.9 15.7 convolution_convert_fusion.2
  1014.0 7.1 fusion.112
  1024.3 5.4 reduce-scatter.14.cloned.1.call-done
  1029.8 44.7 %reduce-scatter.16.cloned.1.call-done = bf16[256,512]{1,0:T(8,128)(2,1)} async-done(((bf16[2048,512]{1,0:T(8,128)(2,1)}), bf16[256,512]{1,0:T(8,128)(2,1)}) %reduce-scatter.16.cloned.1.call-update) | async-done | bytes 262160 | tf_op jit(solution)/shard_map/reduce_scatter | solution.py:86
  1074.5 44.3 %reduce-scatter.18.cloned.1.call-done = bf16[256,512]{1,0:T(8,128)(2,1)} async-done(((bf16[2048,512]{1,0:T(8,128)(2,1)}), bf16[256,512]{1,0:T(8,128)(2,1)}) %reduce-scatter.18.cloned.1.call-update) | async-done | bytes 262160 | tf_op jit(solution)/shard_map/reduce_scatter | solution.py:86
  1118.9 75.6 %reduce-scatter.20.cloned.1.call-done = bf16[256,2048]{1,0:T(8,128)(2,1)} async-done(((bf16[2048,2048]{1,0:T(8,128)(2,1)}), bf16[256,2048]{1,0:T(8,128)(2,1)}) %reduce-scatter.20.cloned.1.call-update) | async-done | bytes 1048592 | tf_op jit(solution)/shard_map/reduce_scatter | solution.py:86
  1194.5 208.7 %reduce-scatter.22.cloned.1.call-done = bf16[256,8192]{1,0:T(8,128)(2,1)} async-done(((bf16[2048,8192]{1,0:T(8,128)(2,1)}), bf16[256,8192]{1,0:T(8,128)(2,1)}) %reduce-scatter.22.cloned.1.call-update) | async-done | bytes 4194320 | tf_op jit(solution)/shard_map/reduce_scatter | solution.py:86
  1403.2 209.1 %reduce-scatter.24.cloned.1.call-done = bf16[256,8192]{1,0:T(8,128)(2,1)} async-done(((bf16[2048,8192]{1,0:T(8,128)(2,1)}), bf16[256,8192]{1,0:T(8,128)(2,1)}) %reduce-scatter.24.cloned.1.call-update) | async-done | bytes 4194320 | tf_op jit(solution)/shard_map/reduce_scatter | solution.py:86
  1612.3 208.8 %reduce-scatter.26.cloned.1.call-done = bf16[1024,2048]{1,0:T(8,128)(2,1)} async-done(((bf16[8192,2048]{1,0:T(8,128)(2,1)}), bf16[1024,2048]{1,0:T(8,128)(2,1)}) %reduce-scatter.26.cloned.1.call-update) | async-done | bytes 4194320 | tf_op jit(solution)/shard_map/reduce_scatter | solution.py:86
  1825.7 14.4 fusion.76
  1840.0 39.9 %all-reduce = (f32[2048]{0:T(1024)}, f32[2048]{0:T(1024)}) all-reduce(f32[2048]{0:T(1024)S(1)} %get-tuple-element.438, f32[2048]{0:T(1024)S(1)} %copy-done.36), channel_id=1, replica_groups=mesh['rep'=4,'shard'=8] {'rep','shard'}, use_global_device_ids=true, to_apply=%region_19.20 | all-reduce | flops 4096 | bytes 32768 | tf_op jit(solution)/shard_map/psum | solution.py:345
  1879.9 6.7 convert_element_type.178
  1886.6 4.9 gather_fusion.1
  1892.7 50.5 %all-gather.36.cloned.1.call-done = bf16[1024,2048]{1,0:T(8,128)(2,1)} async-done(((bf16[256,2048]{1,0:T(8,128)(2,1)}), bf16[1024,2048]{1,0:T(8,128)(2,1)}) %all-gather.36.cloned.1.call-update) | async-done | bytes 4194320 | tf_op jit(solution)/shard_map/all_gather | solution.py:335
  1947.8 477.7 %all-reduce.4.cloned.1.call-done = (bf16[256,512]{1,0:T(8,128)(2,1)}, bf16[256,512]{1,0:T(8,128)(2,1)}, bf16[256,2048]{1,0:T(8,128)(2,1)}, bf16[256,8192]{1,0:T(...) async-done(((bf16[256,512]{1,0:T(8,128)(2,1)}, bf16[256,512]{1,0:T(8,128)(2,1)}, bf16[256,2048]{1,0:T(8,128)(2,1)}, bf16[256,8192]{1,0:T(8,128)(2,1)}, ...) | async-done | bytes 14155792 | tf_op jit(solution)/shard_map/psum | solution.py:338
  2432.0 6.6 convert_element_type.188
  (260 shorter events, 150.9 us)
Async XLA Ops:
  7.2 75.1 %copy-start.34 = (s32[1,1024]{1,0:T(1,128)S(1)}, s32[1,1024]{1,0:T(1,128)}, u32[]{:S(2)}) copy-start(s32[1,1024]{1,0:T(1,128)} %param.29) | copy-start | bytes 12292
  7.2 101.9 %copy-start.27 = (f32[2048]{0:T(1024)S(1)}, f32[2048]{0:T(1024)}, u32[]{:S(2)}) copy-start(f32[2048]{0:T(1024)} %param.20) | copy-start | bytes 24580
  7.2 74.9 %copy-start.41 = (s32[1,3]{1,0:T(1,128)S(1)}, s32[1,3]{1,0:T(1,128)}, u32[]{:S(2)}) copy-start(s32[1,3]{1,0:T(1,128)} %param.30) | copy-start | bytes 40
  7.2 42.2 %all-gather.14.cloned.1.call-start = ((), (), s32[]{:S(2)}) async-start(), calls=%async_computation.9 | async-start | bytes 4718592 | tf_op jit(solution)/shard_map/all_gather | solution.py:137
  7.9 71.3 %all-gather.16.cloned.1.call-start = ((), (), s32[]{:S(2)}) async-start(), calls=%async_computation.10 | async-start | bytes 2359296 | tf_op jit(solution)/shard_map/all_gather | solution.py:144
  8.7 100.4 %all-gather.20.cloned.1.call-start = ((), (), s32[]{:S(2)}) async-start(), calls=%async_computation.12 | async-start | bytes 2359296 | tf_op jit(solution)/shard_map/all_gather | solution.py:143
  9.4 125.5 %all-gather.18.cloned.1.call-start = ((), (), s32[]{:S(2)}) async-start(), calls=%async_computation.11 | async-start | bytes 1179648 | tf_op jit(solution)/shard_map/all_gather | solution.py:162
  53.9 28.6 %copy-start.39 = (f32[128]{0:T(128)}, f32[128]{0:T(128)S(1)}, u32[]{:S(2)}) copy-start(f32[128]{0:T(128)S(1)} %fusion.84) | copy-start | bytes 1540
  53.9 163.1 %copy-start.37 = (f32[128]{0:T(128)}, f32[128]{0:T(128)S(1)}, u32[]{:S(2)}) copy-start(f32[128]{0:T(128)S(1)} %fusion.94) | copy-start | bytes 1540
  82.0 78.8 %all-gather.22.cloned.1.call-start = ((), (), s32[]{:S(2)}) async-start(), calls=%async_computation.13 | async-start | bytes 1179648 | tf_op jit(solution)/shard_map/all_gather | solution.py:161
  82.7 141.2 %copy-start.29 = (f32[128,32]{0,1:T(8,128)}, f32[128,32]{0,1:T(8,128)S(1)}, u32[]{:S(2)}) copy-start(f32[128,32]{0,1:T(8,128)S(1)} %get-tuple-element.540) | copy-start | bytes 49156
  82.7 141.2 %copy-start.31 = (f32[128,32]{0,1:T(8,128)}, f32[128,32]{0,1:T(8,128)S(1)}, u32[]{:S(2)}) copy-start(f32[128,32]{0,1:T(8,128)S(1)} %get-tuple-element.541) | copy-start | bytes 49156
  112.4 104.6 %all-gather.24.cloned.1.call-start = ((), (), s32[]{:S(2)}) async-start(), calls=%async_computation.14 | async-start | bytes 9437184 | tf_op jit(solution)/shard_map/all_gather | solution.py:142
  113.0 161.9 %all-gather.26.cloned.1.call-start = ((), (), s32[]{:S(2)}) async-start(), calls=%async_computation.15 | async-start | bytes 9437184 | tf_op jit(solution)/shard_map/all_gather | solution.py:78
  113.7 322.2 %all-gather.28.cloned.1.call-start = ((), (), s32[]{:S(2)}) async-start(), calls=%async_computation.16 | async-start | bytes 37748736 | tf_op jit(solution)/shard_map/all_gather | solution.py:218
  114.5 484.2 %all-gather.30.cloned.1.call-start = ((), (), s32[]{:S(2)}) async-start(), calls=%async_computation.17 | async-start | bytes 37748736 | tf_op jit(solution)/shard_map/all_gather | solution.py:219
  115.2 646.0 %all-gather.32.cloned.1.call-start = ((), (), s32[]{:S(2)}) async-start(), calls=%async_computation.18 | async-start | bytes 37748736 | tf_op jit(solution)/shard_map/all_gather | solution.py:78
  115.8 799.0 %reduce-scatter.28.cloned.1.call-start = ((), (), s32[]{:S(2)}) async-start(), calls=%async_computation.28 | async-start | bytes 1179648
  280.2 518.8 %copy-start.4 = (f32[128,2048]{1,0:T(8,128)}, f32[128,2048]{1,0:T(8,128)S(1)}, u32[]{:S(2)}) copy-start(f32[128,2048]{1,0:T(8,128)S(1)} %get-tuple-element.543) | copy-start | bytes 3145732
  799.0 18.3 copy-start.18
  817.3 14.0 copy-start.3
  840.3 8.4 copy-start.15
  840.3 8.4 copy-start.22
  860.0 8.4 copy-start.15
  860.1 8.4 copy-start.22
  871.0 15.2 copy-start.30
  871.0 15.2 copy-start.32
  871.0 15.4 copy-start.28
  871.0 15.4 copy-start.38
  878.6 75.8 %reduce-scatter.30.cloned.1.call-start = ((), (), s32[]{:S(2)}) async-start(), calls=%async_computation.29 | async-start | bytes 1179648
  886.2 143.6 %reduce-scatter.14.cloned.1.call-start = ((), (), s32[]{:S(2)}) async-start(), calls=%async_computation.20 | async-start | bytes 9437184 | tf_op jit(solution)/shard_map/reduce_scatter | solution.py:86
  892.4 65.3 %copy-start.7 = (f32[128,2048]{1,0:T(8,128)S(1)}, f32[128,2048]{1,0:T(8,128)}, u32[]{:S(2)}) copy-start(f32[128,2048]{1,0:T(8,128)} %copy-done.6) | copy-start | bytes 3145732
  892.4 65.3 %copy-start.10 = (bf16[128,8,4,64]{0,3,2,1:T(8,128)(2,1)S(1)}, bf16[128,8,4,64]{0,3,2,1:T(8,128)(2,1)}, u32[]{:S(2)}) copy-start(bf16[128,8,4,64]{0,3,2,1:T(8,128)(2,1)} %convert_element_type.161) | copy-start | bytes 1572868
  892.4 182.1 %reduce-scatter.16.cloned.1.call-start = ((), (), s32[]{:S(2)}) async-start(), calls=%async_computation.21 | async-start | bytes 2359296 | tf_op jit(solution)/shard_map/reduce_scatter | solution.py:86
  918.1 200.7 %reduce-scatter.18.cloned.1.call-start = ((), (), s32[]{:S(2)}) async-start(), calls=%async_computation.22 | async-start | bytes 2359296 | tf_op jit(solution)/shard_map/reduce_scatter | solution.py:86
  957.7 236.8 %reduce-scatter.20.cloned.1.call-start = ((), (), s32[]{:S(2)}) async-start(), calls=%async_computation.23 | async-start | bytes 9437184 | tf_op jit(solution)/shard_map/reduce_scatter | solution.py:86
  963.5 439.7 %reduce-scatter.22.cloned.1.call-start = ((), (), s32[]{:S(2)}) async-start(), calls=%async_computation.24 | async-start | bytes 37748736 | tf_op jit(solution)/shard_map/reduce_scatter | solution.py:86
  981.0 631.2 %reduce-scatter.24.cloned.1.call-start = ((), (), s32[]{:S(2)}) async-start(), calls=%async_computation.25 | async-start | bytes 37748736 | tf_op jit(solution)/shard_map/reduce_scatter | solution.py:86
  996.9 824.2 %reduce-scatter.26.cloned.1.call-start = ((), (), s32[]{:S(2)}) async-start(), calls=%async_computation.26 | async-start | bytes 37748736 | tf_op jit(solution)/shard_map/reduce_scatter | solution.py:86
  1013.7 9.3 copy-start.40
  1013.7 866.3 %all-gather.34.cloned.1.call-start = ((), (), s32[]{:S(2)}) async-start(), calls=%async_computation.19 | async-start | bytes 4718592 | tf_op jit(solution)/shard_map/all_gather | solution.py:330
  1024.3 796.9 %copy-start.35 = (s32[1,1024]{1,0:T(1,128)S(1)}, s32[1,1024]{1,0:T(1,128)}, u32[]{:S(2)}) copy-start(s32[1,1024]{1,0:T(1,128)} %param.29) | copy-start | bytes 12292
  1024.3 801.4 %copy-start.5 = (f32[128,2048]{1,0:T(8,128)S(1)}, f32[128,2048]{1,0:T(8,128)}, u32[]{:S(2)}) copy-start(f32[128,2048]{1,0:T(8,128)} %copy-done.4) | copy-start | bytes 3145732
  1024.3 801.4 %copy-start.9 = (bf16[128,8192]{1,0:T(8,128)(2,1)S(1)}, bf16[128,8192]{1,0:T(8,128)(2,1)}, u32[]{:S(2)}) copy-start(bf16[128,8192]{1,0:T(8,128)(2,1)} %get-tuple-element.530) | copy-start | bytes 6291460
  1024.3 918.9 %all-gather.36.cloned.1.call-start = ((), (), s32[]{:S(2)}) async-start(), calls=%async_computation.27 | async-start | bytes 5242880 | tf_op jit(solution)/shard_map/all_gather | solution.py:335
  1029.8 1395.7 %all-reduce.4.cloned.1.call-start = ((), (), s32[]{:S(2)}) async-start(), calls=%async_computation.30 | async-start | bytes 28311552 | tf_op jit(solution)/shard_map/psum | solution.py:338
  1825.6 14.4 copy-start.36
  2427.3 11.3 copy-start.12
  (27 other events, 125.8 us)
Sparse Core Ops, SparseCore 0:
  9.9 39.4 all-gather.13
  51.3 27.8 all-gather.15
  81.1 27.9 all-gather.19
  111.4 23.4 all-gather.17
  137.2 23.5 all-gather.21
  162.5 54.3 all-gather.23
  218.8 54.4 all-gather.25
  275.2 160.7 all-gather.27
  437.9 160.7 all-gather.29
  600.4 160.7 all-gather.31
  878.7 36.0 reduce-scatter.27
  918.4 35.9 reduce-scatter.29
  958.5 71.2 reduce-scatter.13
  1033.3 41.2 reduce-scatter.15
  1077.6 41.1 reduce-scatter.17
  1123.1 71.2 reduce-scatter.19
  1197.9 205.2 reduce-scatter.21
  1407.0 205.2 reduce-scatter.23
  1615.9 205.2 reduce-scatter.25
  1823.6 37.2 all-gather.33
  1862.5 80.5 all-gather.35
  1946.8 478.6 all-reduce.3
